TPU v7x, 32 devices: a whole 2x2x4 slice. The times are simulated.
32 devices in a mesh: dp: 8 (over y, x, core), tensor: 4 (over z).
Axes of the slice: x: 2, y: 2, z: 4, core: 2. Of those that a mesh axis runs over, the one named last changes fastest.
Arguments:
- latents: bfloat16 [16384, 1280], P('dp'), may hold values from -6 to 6
- norm1_gain: float32 [1280], replicated, may hold values from 0.5 to 1.5
- norm1_shift: float32 [1280], replicated, may hold values from -1.75 to 1.75
- query_weight: bfloat16 [1280, 1280], P(None, 'tensor'), may hold values from -0.15625 to 0.15625
- query_bias: float32 [1280], P('tensor'), may hold values from -1.75 to 1.75
- key_weight: bfloat16 [1280, 1280], P(None, 'tensor'), may hold values from -0.15625 to 0.15625
- value_weight: bfloat16 [1280, 1280], P(None, 'tensor'), may hold values from -0.15625 to 0.15625
- value_bias: float32 [1280], P('tensor'), may hold values from -1.75 to 1.75
- out_weight: bfloat16 [1280, 1280], P('tensor'), may hold values from -0.625 to 0.625
- out_bias: float32 [1280], replicated, may hold values from -1.75 to 1.75
- norm2_gain: float32 [1280], replicated, may hold values from 0.5 to 1.5
- norm2_shift: float32 [1280], replicated, may hold values from -1.75 to 1.75
- hidden_weight: bfloat16 [1280, 1280], P(None, 'tensor'), may hold values from -0.15625 to 0.15625
- hidden_bias: float32 [1280], P('tensor'), may hold values from -1.75 to 1.75
- proj_weight: bfloat16 [1280, 1280], P('tensor'), may hold values from -0.25 to 0.25
- proj_bias: float32 [1280], replicated, may hold values from -1.75 to 1.75
- segments: int32 [16, 1024], P('dp'), may hold values from 0 to 7, never falling along the last dimension, each value on 1 to 512 neighbouring positions
- valid_mask: int32 [16, 1024], P('dp'), may hold values 0 or 1
- cotangent: bfloat16 [16384, 1280], P('dp'), may hold values from -6 to 6
Outputs:
- output: bfloat16 [16384, 1280], P('dp')
- grad_input: float32 [16384, 1280], P('dp')
- grad_norm1_gain: float32 [1280], replicated
- grad_norm1_shift: float32 [1280], replicated
- grad_query_weight: float32 [1280, 1280], P(None, 'tensor')
- grad_query_bias: float32 [1280], P('tensor')
- grad_key_weight: float32 [1280, 1280], P(None, 'tensor')
- grad_value_weight: float32 [1280, 1280], P(None, 'tensor')
- grad_value_bias: float32 [1280], P('tensor')
- grad_out_weight: float32 [1280, 1280], P('tensor')
- grad_out_bias: float32 [1280], replicated
- grad_norm2_gain: float32 [1280], replicated
- grad_norm2_shift: float32 [1280], replicated
- grad_hidden_weight: float32 [1280, 1280], P(None, 'tensor')
- grad_hidden_bias: float32 [1280], P('tensor')
- grad_proj_weight: float32 [1280, 1280], P('tensor')
- grad_proj_bias: float32 [1280], replicated
- rms: float32 [16, 3], P('dp')
Inputs may be any that keep to these rules, and one draw needn't show every extreme that they name: `segments`: in each row segment numbers never fall, each document has 1 to 512 positions, and one has exactly that many.
All inputs are finite; a program needn't handle non-finite values. No bound on the sum of `valid_mask` on one device may be relied on, other than what follows from the above.
Results may differ from a plain program's by a relative error of at most 0.013.
Values sent between devices are 32-bit elements; how exact they have to be, the bound alone decides.
A program may use at most 192 MiB of HBM per device.

v0:
```python
import math
import jax
import jax.numpy as jnp
from jax import lax
from jax.sharding import PartitionSpec as P

HEAD_DIM = 160
EPS = 1e-05
NEG = -1e30


def layer_norm(v, gain, shift):
    center = v - jnp.mean(v, axis=-1, keepdims=True)
    spread = jnp.mean(center * center, axis=-1, keepdims=True)
    return center * lax.rsqrt(spread + EPS) * gain + shift


def inner(left, right):
    return lax.dot_general(
        left, right, (((0,), (0,)), ((), ())), preferred_element_type=jnp.float32
    )


def outer(left, right):
    return lax.dot_general(
        left, right, (((1,), (1,)), ((), ())), preferred_element_type=jnp.float32
    )


def mask_of(seg):
    length = seg.shape[0]
    rowpos = lax.broadcasted_iota(jnp.int32, (length, length), 0)
    colpos = lax.broadcasted_iota(jnp.int32, (length, length), 1)
    return ((rowpos >= colpos) & (seg[:, None] == seg[None, :]))[None]


def scores_of(query, keyed, seg):
    scores = jnp.einsum(
        "qhe,khe->hqk", query, keyed, preferred_element_type=jnp.float32
    ) / math.sqrt(HEAD_DIM)
    allowed = mask_of(seg)
    return (jnp.where(allowed, scores, NEG), allowed)


def attend_forward(query, keyed, valued, seg):
    scores, allowed = scores_of(query, keyed, seg)
    top = jnp.max(scores, axis=-1, keepdims=True)
    weights = jnp.where(allowed, jnp.exp(scores - top), 0.0)
    total = jnp.sum(weights, axis=-1, keepdims=True)
    probs = (weights / total).astype(jnp.bfloat16)
    mixed = jnp.einsum("hqk,khe->qhe", probs, valued, preferred_element_type=jnp.float32).astype(
        jnp.bfloat16
    )
    return (mixed, (top + jnp.log(total))[..., 0])


def attend_backward(query, keyed, valued, seg, logsum, d_mixed):
    scores, allowed = scores_of(query, keyed, seg)
    probs = jnp.where(allowed, jnp.exp(scores - logsum[..., None]), 0.0)
    low_probs = probs.astype(jnp.bfloat16)
    d_valued = jnp.einsum(
        "hqk,qhe->khe", low_probs, d_mixed, preferred_element_type=jnp.float32
    ).astype(jnp.bfloat16)
    d_probs = jnp.einsum("qhe,khe->hqk", d_mixed, valued, preferred_element_type=jnp.float32)
    d_scores = probs * (d_probs - jnp.sum(probs * d_probs, axis=-1, keepdims=True))
    low_scores = d_scores.astype(jnp.bfloat16)
    scale = 1.0 / math.sqrt(HEAD_DIM)
    d_query = (
        jnp.einsum("hqk,khe->qhe", low_scores, keyed, preferred_element_type=jnp.float32) * scale
    ).astype(jnp.bfloat16)
    d_keyed = (
        jnp.einsum("hqk,qhe->khe", low_scores, query, preferred_element_type=jnp.float32) * scale
    ).astype(jnp.bfloat16)
    return (d_query, d_keyed, d_valued)


def shards(
    latents,
    norm1_gain,
    norm1_shift,
    query_weight,
    query_bias,
    key_weight,
    value_weight,
    value_bias,
    out_weight,
    out_bias,
    norm2_gain,
    norm2_shift,
    hidden_weight,
    hidden_bias,
    proj_weight,
    proj_bias,
    segments,
    valid_mask,
    cotangent,
):
    seq_count, length = segments.shape
    tok_rows, width = latents.shape
    local_heads = query_weight.shape[1] // HEAD_DIM

    def split(t):
        return t.reshape(seq_count, length, local_heads, HEAD_DIM)

    inputs = latents.astype(jnp.float32)
    normed1 = layer_norm(inputs, norm1_gain, norm1_shift).astype(jnp.bfloat16)
    query = (
        jnp.dot(normed1, query_weight, preferred_element_type=jnp.float32) + query_bias
    ).astype(jnp.bfloat16)
    keyed = jnp.dot(normed1, key_weight, preferred_element_type=jnp.float32).astype(jnp.bfloat16)
    valued = (
        jnp.dot(normed1, value_weight, preferred_element_type=jnp.float32) + value_bias
    ).astype(jnp.bfloat16)
    mixed, logsum = lax.map(
        lambda t: attend_forward(t[0], t[1], t[2], t[3]),
        (split(query), split(keyed), split(valued), segments),
    )
    mixed = mixed.reshape(tok_rows, local_heads * HEAD_DIM)
    attended = (
        lax.psum(jnp.dot(mixed, out_weight, preferred_element_type=jnp.float32), "tensor")
        + out_bias
    )
    resid = inputs + attended
    normed2 = layer_norm(resid, norm2_gain, norm2_shift).astype(jnp.bfloat16)
    pre = jnp.dot(normed2, hidden_weight, preferred_element_type=jnp.float32) + hidden_bias
    act = jax.nn.gelu(pre, approximate=False).astype(jnp.bfloat16)
    branch = (
        lax.psum(jnp.dot(act, proj_weight, preferred_element_type=jnp.float32), "tensor")
        + proj_bias
    )
    output = resid + branch
    weight = valid_mask.astype(jnp.float32)
    counted = jnp.maximum(jnp.sum(weight, axis=1), 1.0) * width

    def per_seq(v):
        return jnp.sum(weight * jnp.sum(v * v, axis=-1).reshape(seq_count, length), axis=1)

    stat_sums = jnp.stack([per_seq(attended), per_seq(branch), per_seq(output)], axis=1)
    rms = jnp.sqrt(stat_sums / counted[:, None])
    grad_out = cotangent.astype(jnp.float32)
    grad_w2 = inner(act, cotangent)
    grad_b2 = jnp.sum(grad_out, axis=0)
    d_act = outer(cotangent, proj_weight)
    d_pre = jax.vjp(lambda t: jax.nn.gelu(t, approximate=False), pre)[1](d_act)[0]
    low_pre = d_pre.astype(jnp.bfloat16)
    grad_w1 = inner(normed2, low_pre)
    grad_b1 = jnp.sum(low_pre.astype(jnp.float32), axis=0)
    d_normed2 = lax.psum(outer(low_pre, hidden_weight), "tensor")
    norm_back2 = jax.vjp(layer_norm, resid, norm2_gain, norm2_shift)[1]
    d_resid_norm, grad_g2, grad_c2 = norm_back2(d_normed2)
    d_resid = grad_out + d_resid_norm
    low_attended = d_resid.astype(jnp.bfloat16)
    grad_bo = jnp.sum(low_attended.astype(jnp.float32), axis=0)
    grad_wo = inner(mixed, low_attended)
    d_mixed = outer(low_attended, out_weight).astype(jnp.bfloat16)
    d_query, d_keyed, d_valued = lax.map(
        lambda t: attend_backward(t[0], t[1], t[2], t[3], t[4], t[5]),
        (split(query), split(keyed), split(valued), segments, logsum, split(d_mixed)),
    )
    d_query = d_query.reshape(tok_rows, local_heads * HEAD_DIM)
    d_keyed = d_keyed.reshape(tok_rows, local_heads * HEAD_DIM)
    d_valued = d_valued.reshape(tok_rows, local_heads * HEAD_DIM)
    grad_wq = inner(normed1, d_query)
    grad_bq = jnp.sum(d_query.astype(jnp.float32), axis=0)
    grad_wk = inner(normed1, d_keyed)
    grad_wv = inner(normed1, d_valued)
    grad_bv = jnp.sum(d_valued.astype(jnp.float32), axis=0)
    partial_in = (
        outer(d_query, query_weight) + outer(d_keyed, key_weight) + outer(d_valued, value_weight)
    )
    d_normed1 = lax.psum(partial_in, "tensor")
    norm_back1 = jax.vjp(layer_norm, inputs, norm1_gain, norm1_shift)[1]
    d_input_norm, grad_g1, grad_c1 = norm_back1(d_normed1)
    grad_input = d_resid + d_input_norm
    (
        grad_g1,
        grad_c1,
        grad_wq,
        grad_bq,
        grad_wk,
        grad_wv,
        grad_bv,
        grad_wo,
        grad_bo,
        grad_g2,
        grad_c2,
        grad_w1,
        grad_b1,
        grad_w2,
        grad_b2,
    ) = lax.psum(
        (
            grad_g1,
            grad_c1,
            grad_wq,
            grad_bq,
            grad_wk,
            grad_wv,
            grad_bv,
            grad_wo,
            grad_bo,
            grad_g2,
            grad_c2,
            grad_w1,
            grad_b1,
            grad_w2,
            grad_b2,
        ),
        "dp",
    )
    return (
        output.astype(jnp.bfloat16),
        grad_input,
        grad_g1,
        grad_c1,
        grad_wq,
        grad_bq,
        grad_wk,
        grad_wv,
        grad_bv,
        grad_wo,
        grad_bo,
        grad_g2,
        grad_c2,
        grad_w1,
        grad_b1,
        grad_w2,
        grad_b2,
        rms,
    )


def solution(mesh):
    placed = (
        P("dp", None),
        P(),
        P(),
        P(None, "tensor"),
        P("tensor"),
        P(None, "tensor"),
        P(None, "tensor"),
        P("tensor"),
        P("tensor", None),
        P(),
        P(),
        P(),
        P(None, "tensor"),
        P("tensor"),
        P("tensor", None),
        P(),
        P("dp", None),
        P("dp", None),
        P("dp", None),
    )
    return jax.shard_map(
        shards,
        mesh=mesh,
        in_specs=placed,
        out_specs=(
            P("dp", None),
            P("dp", None),
            P(),
            P(),
            P(None, "tensor"),
            P("tensor"),
            P(None, "tensor"),
            P(None, "tensor"),
            P("tensor"),
            P("tensor", None),
            P(),
            P(),
            P(),
            P(None, "tensor"),
            P("tensor"),
            P("tensor", None),
            P(),
            P("dp", None),
        ),
        check_vma=False,
    )
```

profile of v0, /device:TPU:0, one launch (start us, length us, event | category | flops | bytes accessed | tf_op | source)
XLA Modules:
  0.0 1821.8 jit_solution(10788580656488504458)
XLA Ops:
  21.8 5.4 fusion.71
  32.3 4.4 fusion.70
  41.4 20.8 %while.26 = (s32[]{:T(128)}, bf16[2,1024,2,160]{1,3,2,0:T(8,128)(2,1)}, f32[2,2,1024]{2,1,0:T(2,128)S(1)}, bf16[2,1024,2,160]{1,3,2,0:T(8,128)(2,1)S(1)}, s32[2,...) while((s32[]{:T(128)}, ...), condition=%wide.region_5.6_spmd, body=%wide.region_2.5_spmd.sunk | while | flops 1375008768 | bytes 42547356 | solution.py:114
  62.2 3.6 copy.56
  67.3 5.7 fusion.87
  73.5 360.7 %all-reduce.8.cloned.1.call-done = f32[2048,1280]{1,0:T(8,128)} async-done(((f32[2048,1280]{1,0:T(8,128)}), f32[2048,1280]{1,0:T(8,128)}) %all-reduce.8.cloned.1.call-update) | async-done | bytes 10485776 | tf_op jit(solution)/shard_map/psum | solution.py:120
  434.3 11.8 fusion.86
  446.1 5.3 multiply_reduce_fusion.6
  459.3 10.2 convert_reduce_fusion.3
  470.1 5.5 fusion.88
  475.6 5.4 fusion.89
  481.3 697.6 %all-reduce.14.cloned.1.call-done = (f32[2048,1280]{1,0:T(8,128)}, f32[2048,1280]{1,0:T(8,128)}) async-done(((f32[2048,1280]{1,0:T(8,128)}, f32[2048,1280]{1,0:T(8,128)}), (f32[2048,1280]{1,0:T(8,128)}, f32[2048,1280]{1,0:T(8,128)})) %all-reduce.14.cloned.1.call-update) | async-done | bytes 20971536 | tf_op jit(solution)/shard_map/psum | solution.py:128
  1179.0 15.7 multiply_reduce_fusion.2
  1196.9 3.9 fusion.85
  1200.9 7.7 convert_reduce_fusion.2
  1220.0 55.4 %while.27 = (s32[]{:T(128)}, bf16[2,1024,2,160]{1,3,2,0:T(8,128)(2,1)}, bf16[2,1024,2,160]{1,3,2,0:T(8,128)(2,1)}, bf16[2,1024,2,160]{1,3,2,0:T(8,128)(2,1)}, bf...) while((s32[]{:T(128)}, ...), condition=%wide.region_15.16_spmd, body=%wide.region_13.15_spmd.sunk | while | flops 3381196800 | bytes 147121552 | solution.py:156
  1223.5 6.0 multiply_reduce_fusion.11
  1229.6 8.2 multiply_convert_fusion.3
  1237.8 6.0 fusion.171
  1250.9 6.0 multiply_reduce_fusion.11
  1257.0 8.2 multiply_convert_fusion.3
  1265.2 6.0 fusion.171
  1289.1 9.0 add_add_fusion.3
  1299.5 5.7 fusion.97
  1308.5 5.7 fusion.92
  1314.2 5.7 fusion.96
  1328.3 327.4 %all-reduce.10.cloned.1.call-done = f32[2048,1280]{1,0:T(8,128)} async-done(((f32[2048,1280]{1,0:T(8,128)}), f32[2048,1280]{1,0:T(8,128)}) %all-reduce.10.cloned.1.call-update) | async-done | bytes 10485776 | tf_op jit(solution)/shard_map/psum | solution.py:171
  1655.7 7.9 fusion.82
  1663.7 9.8 fusion.65
  1673.7 12.9 convert_reduce_fusion.1
  1686.5 26.9 %all-reduce = (f32[1280]{0:T(1024)}, f32[1280]{0:T(1024)}, f32[320]{0:T(512)}, f32[320]{0:T(512)}, f32[1280]{0:T(1024)}, /*index=5*/f32[1280]{0:T(1024)}, f32[1280]{0:T(1024)}, f32[320]{0:T(512)}, f32[1280]{0:T(1024)}) all-reduce(f32[1280]{0:T(1024)S(1)} %get-tuple-element.187, ...), channel_id=1, replica_groups=mesh['dp'=8,'tensor'=4] {'dp'}, use_global_device_ids=true, to_apply=%region_20.21 | all-reduce | flops 8640 | bytes 69120 | tf_op jit(solution)/shard_map/psum | solution.py:191
  1713.5 92.8 %all-reduce.12.cloned.1.call-done = (f32[1280,320]{0,1:T(8,128)}, f32[1280,320]{0,1:T(8,128)}, f32[1280,320]{0,1:T(8,128)}, f32[320,1280]{1,0:T(8,128)}, f32[1280,320]{0,1:T(8,128)}, /*index=5*/f32[320,1280]{1,0:T(8,128)}) async-done(((f32[1280,320]{0,1:T(8,128)}, f32[1280,320]{0,1:T(8,128)}, f32[1280,320]{0,1:T(8,128)}, f32[320,1280]{1,0:T(8,128)}, f32[1280,320]{0,1:T(8,128)}, ...) | async-done | bytes 9830416 | tf_op jit(solution)/shard_map/psum | solution.py:191
  (306 shorter events, 118.4 us)
Async XLA Ops:
  7.2 450.7 %copy-start = (bf16[320,1280]{1,0:T(8,128)(2,1)S(1)}, bf16[320,1280]{1,0:T(8,128)(2,1)}, u32[]{:S(2)}) copy-start(bf16[320,1280]{1,0:T(8,128)(2,1)} %param.37) | copy-start | bytes 2457604
  7.2 427.1 %all-reduce.8.cloned.1.call-start = ((), (), s32[]{:S(2)}) async-start(), calls=%async_computation | async-start | bytes 20971520 | tf_op jit(solution)/shard_map/psum | solution.py:120
  72.9 361.3 %copy-start.69 = (f32[1280]{0:T(1024)S(1)}, f32[1280]{0:T(1024)}, u32[]{:S(2)}) copy-start(f32[1280]{0:T(1024)} %param.32) | copy-start | bytes 15364
  73.0 1106.0 %all-reduce.14.cloned.1.call-start = ((), (), s32[]{:S(2)}) async-start(), calls=%async_computation.3 | async-start | bytes 41943040 | tf_op jit(solution)/shard_map/psum | solution.py:128
  481.0 697.9 %copy-start.71 = (f32[1280]{0:T(1024)S(1)}, f32[1280]{0:T(1024)}, u32[]{:S(2)}) copy-start(f32[1280]{0:T(1024)} %param.38) | copy-start | bytes 15364
  481.1 1174.7 %all-reduce.10.cloned.1.call-start = ((), (), s32[]{:S(2)}) async-start(), calls=%async_computation.1 | async-start | bytes 20971520 | tf_op jit(solution)/shard_map/psum | solution.py:171
  1178.9 15.8 slice-start
  1178.9 15.8 slice-start.8
  1178.9 15.8 slice-start.1
  1178.9 16.2 slice-start.2
  1179.0 17.4 slice-start.9
  1179.0 18.0 slice-start.10
  1200.8 7.8 copy-start.5
  1200.8 7.8 copy-start.58
  1200.8 10.1 copy-start.45
  1298.2 7.0 slice-start.13
  1298.2 508.1 %all-reduce.12.cloned.1.call-start = ((), (), s32[]{:S(2)}) async-start(), calls=%async_computation.2 | async-start | bytes 19660800 | tf_op jit(solution)/shard_map/psum | solution.py:191
  1308.5 11.4 slice-start.15
  1326.0 329.7 %copy-start.51 = (f32[2048]{0:T(1024)S(1)}, f32[2048]{0:T(1024)}, u32[]{:S(2)}) copy-start(f32[2048]{0:T(1024)} %copy-done.50) | copy-start | bytes 24580
  1326.0 329.7 %copy-start.54 = (f32[1280]{0:T(1024)S(1)}, f32[1280]{0:T(1024)}, u32[]{:S(2)}) copy-start(f32[1280]{0:T(1024)} %param.24) | copy-start | bytes 15364
  1328.3 335.3 %copy-start.61 = (f32[2048]{0:T(1024)S(1)}, f32[2048]{0:T(1024)}, u32[]{:S(2)}) copy-start(f32[2048]{0:T(1024)} %copy-done.60) | copy-start | bytes 24580
  1328.3 335.4 %copy-start.56 = (f32[2048]{0:T(1024)S(1)}, f32[2048]{0:T(1024)}, u32[]{:S(2)}) copy-start(f32[2048]{0:T(1024)} %copy-done.55) | copy-start | bytes 24580
  1655.7 17.8 slice-start.5
  1655.7 17.8 slice-start.6
  1663.7 9.9 slice-start.3
  1663.7 9.9 slice-start.4
  1663.7 9.9 slice-start.7
  1663.7 9.9 copy-start.59
  1673.6 12.9 copy-start.62
  1673.6 12.9 copy-start.63
  1673.6 12.9 copy-start.64
  1673.7 12.9 copy-start.73
  (77 other events, 252.5 us)
Sparse Core Ops, SparseCore 0:
  73.1 361.1 all-reduce.7
  481.2 697.6 all-reduce.13
  1298.3 357.3 all-reduce.9
  1662.1 144.1 all-reduce.11
where the time goes:
time: 1830 us; the launch traced here: 1820 us
  waiting for transfers between devices  1480 us (81%)
  matrix products  130 us (7%)
  other arithmetic  109 us (6%)
  local copies, waits for them, and re-layouts  60.1 us (3%)
  blocking collectives  26.9 us (1%)
    psum x1, waiting for transfers between devices, shards(): lax.psum(jnp.dot(act, proj_weight, preferred_element_type=jnp.float32), '...  698 us
    psum x1, waiting for transfers between devices, shards(): lax.psum(jnp.dot(mixed, out_weight, preferred_element_type=jnp.float32),...  361 us
    psum x1, waiting for transfers between devices, shards(): d_normed1 = lax.psum(partial_in, 'tensor')  327 us
    psum x1, waiting for transfers between devices, shards(): lax.psum((grad_g1, grad_c1, grad_wq, grad_bq, grad_wk, grad_wv, grad_bv,...  92.8 us
  transfers between devices with their start and end apart: 4, of which 4 were waited for; matrix products, arithmetic and copies ran while one was open for 3% of the time, Pallas kernels for 0%

commit v1 on v0

--- a/solution.py
+++ b/solution.py
@@ -168,7 +168,11 @@
     partial_in = (
         outer(d_query, query_weight) + outer(d_keyed, key_weight) + outer(d_valued, value_weight)
     )
-    d_normed1 = lax.psum(partial_in, "tensor")
+    d_normed1 = partial_in
+    for hop in (1, 2):
+        d_normed1 = d_normed1 + lax.ppermute(
+            d_normed1, "tensor", [(dev, dev ^ hop) for dev in range(4)]
+        )
     norm_back1 = jax.vjp(layer_norm, inputs, norm1_gain, norm1_shift)[1]
     d_input_norm, grad_g1, grad_c1 = norm_back1(d_normed1)
     grad_input = d_resid + d_input_norm

time: 1830 us -> 2070 us (1.13)
  waiting for transfers between devices: 1480 us -> 1710 us
    ppermute x0 -> x2, waiting for transfers between devices: none -> 647 us  [shards(): lax.ppermute(d_normed1, 'tensor', [(dev, dev ^ hop) for dev in range(4)])]
    psum x1 -> x0, waiting for transfers between devices: 327 us -> none  [shards(): d_normed1 = lax.psum(partial_in, 'tensor')]
    psum x1, waiting for transfers between devices: 92.8 us -> 0.01 us  [shards(): lax.psum((grad_g1, grad_c1, grad_wq, grad_bq, grad_wk, grad_wv, grad_bv,...]
  transfers between devices with their start and end apart: 4 -> 5, of which waited for: 4 -> 4; matrix products, arithmetic and copies ran while one was open for 3% -> 3% of each run, Pallas kernels for 0% -> 0%
where the time goes in v1:
time: 2070 us; the launch traced here: 2060 us
  waiting for transfers between devices  1710 us (83%)
  matrix products  133 us (6%)
  other arithmetic  116 us (6%)
  local copies, waits for them, and re-layouts  58.7 us (3%)
  blocking collectives  25.2 us (1%)
    psum x1, waiting for transfers between devices, shards(): lax.psum(jnp.dot(act, proj_weight, preferred_element_type=jnp.float32), '...  698 us
    ppermute x2, waiting for transfers between devices, shards(): lax.ppermute(d_normed1, 'tensor', [(dev, dev ^ hop) for dev in range(4)])  647 us
    psum x1, waiting for transfers between devices, shards(): lax.psum(jnp.dot(mixed, out_weight, preferred_element_type=jnp.float32),...  361 us
  transfers between devices with their start and end apart: 5, of which 4 were waited for; matrix products, arithmetic and copies ran while one was open for 3% of the time, Pallas kernels for 0%

profile of v1, /device:TPU:0, one launch (start us, length us, event | category | flops | bytes accessed | tf_op | source)
XLA Modules:
  0.0 2056.6 jit_solution(8976273735499108372)
XLA Ops:
  21.8 5.4 fusion.71
  32.3 4.4 fusion.70
  41.4 20.8 %while.26 = (s32[]{:T(128)}, bf16[2,1024,2,160]{1,3,2,0:T(8,128)(2,1)}, f32[2,2,1024]{2,1,0:T(2,128)S(1)}, bf16[2,1024,2,160]{1,3,2,0:T(8,128)(2,1)S(1)}, s32[2,...) while((s32[]{:T(128)}, ...), condition=%wide.region_5.6_spmd, body=%wide.region_2.5_spmd.sunk | while | flops 1375008768 | bytes 42547356 | solution.py:114
  67.3 5.7 fusion.87
  73.5 360.7 %all-reduce.7.cloned.1.call-done = f32[2048,1280]{1,0:T(8,128)} async-done(((f32[2048,1280]{1,0:T(8,128)}), f32[2048,1280]{1,0:T(8,128)}) %all-reduce.7.cloned.1.call-update) | async-done | bytes 10485776 | tf_op jit(solution)/shard_map/psum | solution.py:120
  434.3 11.8 fusion.86
  446.1 5.3 multiply_reduce_fusion.6
  459.3 10.2 convert_reduce_fusion.3
  470.1 5.5 fusion.88
  475.6 5.5 fusion.89
  481.3 697.6 %all-reduce.11.cloned.1.call-done = (f32[2048,1280]{1,0:T(8,128)}, f32[2048,1280]{1,0:T(8,128)}) async-done(((f32[2048,1280]{1,0:T(8,128)}, f32[2048,1280]{1,0:T(8,128)}), (f32[2048,1280]{1,0:T(8,128)}, f32[2048,1280]{1,0:T(8,128)})) %all-reduce.11.cloned.1.call-update) | async-done | bytes 20971536 | tf_op jit(solution)/shard_map/psum | solution.py:128
  1179.0 15.7 multiply_reduce_fusion.2
  1200.9 7.7 convert_reduce_fusion.2
  1220.0 55.4 %while.27 = (s32[]{:T(128)}, bf16[2,1024,2,160]{1,3,2,0:T(8,128)(2,1)}, bf16[2,1024,2,160]{1,3,2,0:T(8,128)(2,1)}, bf16[2,1024,2,160]{1,3,2,0:T(8,128)(2,1)}, bf...) while((s32[]{:T(128)}, ...), condition=%wide.region_15.16_spmd, body=%wide.region_13.15_spmd.sunk | while | flops 3381196800 | bytes 147121552 | solution.py:156
  1223.6 6.0 multiply_reduce_fusion.11
  1229.6 8.2 multiply_convert_fusion.3
  1237.8 6.0 fusion.171
  1251.0 6.0 multiply_reduce_fusion.11
  1257.0 8.2 multiply_convert_fusion.3
  1265.2 6.0 fusion.171
  1289.1 9.0 add_add_fusion.3
  1298.2 227.4 %collective-permute-done = f32[2048,1280]{1,0:T(8,128)} collective-permute-done((f32[2048,1280]{1,0:T(8,128)}, f32[2048,1280]{1,0:T(8,128)}, u32[]{:S(2)}, u32[]{:S(2)}) %collective-permute-start) | collective-permute-done | bytes 10485792 | tf_op jit(solution)/shard_map/ppermute | solution.py:173
  1525.6 12.4 add.180
  1539.3 5.6 fusion.97
  1544.9 5.6 fusion.93
  1550.6 5.7 fusion.92
  1556.3 5.7 fusion.96
  1570.7 419.5 %collective-permute-done.1 = f32[2048,1280]{1,0:T(8,128)} collective-permute-done((f32[2048,1280]{1,0:T(8,128)}, f32[2048,1280]{1,0:T(8,128)}, u32[]{:S(2)}, u32[]{:S(2)}) %collective-permute-start.1) | collective-permute-done | bytes 10485792 | tf_op jit(solution)/shard_map/ppermute | solution.py:173
  1990.2 9.7 fusion.82
  2000.0 5.2 fusion.65
  2005.3 10.6 convert_reduce_fusion.1
  2015.9 25.2 %all-reduce = (f32[1280]{0:T(1024)}, f32[1280]{0:T(1024)}, f32[320]{0:T(512)}, f32[320]{0:T(512)}, f32[1280]{0:T(1024)}, /*index=5*/f32[1280]{0:T(1024)}, f32[1280]{0:T(1024)}, f32[320]{0:T(512)}, f32[1280]{0:T(1024)}) all-reduce(f32[1280]{0:T(1024)S(1)} %get-tuple-element.187, ...), channel_id=1, replica_groups=mesh['dp'=8,'tensor'=4] {'dp'}, use_global_device_ids=true, to_apply=%region_19.20 | all-reduce | flops 8640 | bytes 69120 | tf_op jit(solution)/shard_map/psum | solution.py:195
  (301 shorter events, 122.9 us)
Async XLA Ops:
  7.2 450.7 %copy-start = (bf16[320,1280]{1,0:T(8,128)(2,1)S(1)}, bf16[320,1280]{1,0:T(8,128)(2,1)}, u32[]{:S(2)}) copy-start(bf16[320,1280]{1,0:T(8,128)(2,1)} %param.37) | copy-start | bytes 2457604
  7.2 427.1 %all-reduce.7.cloned.1.call-start = ((), (), s32[]{:S(2)}) async-start(), calls=%async_computation | async-start | bytes 20971520 | tf_op jit(solution)/shard_map/psum | solution.py:120
  72.9 361.3 %copy-start.69 = (f32[1280]{0:T(1024)S(1)}, f32[1280]{0:T(1024)}, u32[]{:S(2)}) copy-start(f32[1280]{0:T(1024)} %param.32) | copy-start | bytes 15364
  73.0 1106.0 %all-reduce.11.cloned.1.call-start = ((), (), s32[]{:S(2)}) async-start(), calls=%async_computation.2 | async-start | bytes 41943040 | tf_op jit(solution)/shard_map/psum | solution.py:128
  446.1 7.0 copy-start.57
  446.1 7.0 copy-start.70
  481.1 697.9 %copy-start.71 = (f32[1280]{0:T(1024)S(1)}, f32[1280]{0:T(1024)}, u32[]{:S(2)}) copy-start(f32[1280]{0:T(1024)} %param.38) | copy-start | bytes 15364
  481.1 1560.1 %all-reduce.9.cloned.1.call-start = ((), (), s32[]{:S(2)}) async-start(), calls=%async_computation.1 | async-start | bytes 19660800 | tf_op jit(solution)/shard_map/psum | solution.py:195
  1179.0 15.8 slice-start
  1179.0 15.8 slice-start.5
  1179.0 15.8 slice-start.1
  1179.0 16.2 slice-start.2
  1179.0 17.4 slice-start.6
  1179.0 18.0 slice-start.7
  1200.8 7.8 copy-start.5
  1200.9 7.8 copy-start.58
  1200.9 10.1 copy-start.45
  1298.2 241.1 %copy-start.65 = (f32[2048]{0:T(1024)S(1)}, f32[2048]{0:T(1024)}, u32[]{:S(2)}) copy-start(f32[2048]{0:T(1024)} %get-tuple-element.266) | copy-start | bytes 24580
  1298.2 241.1 %copy-start.35 = (bf16[2048,320]{0,1:T(8,128)(2,1)S(1)}, bf16[2048,320]{0,1:T(8,128)(2,1)}, u32[]{:S(2)}) copy-start(bf16[2048,320]{0,1:T(8,128)(2,1)} %copy-done.34) | copy-start | bytes 3932164
  1298.2 227.5 %collective-permute-start = (f32[2048,1280]{1,0:T(8,128)}, f32[2048,1280]{1,0:T(8,128)}, u32[]{:S(2)}, u32[]{:S(2)}) collective-permute-start(f32[2048,1280]{1,0:T(8,128)} %add_add_fusion.3), channel_id=1, source_target_pairs={{0,1},{1,0},{2,3},{3,2},{4,5},{5,4},{6,7},{7,6},{8,9},{9,8},{10,11... | collective-permute-start | bytes 31457288 | tf_op jit(solution)/shard_map/ppermute | solution.py:173
  1538.0 452.2 %collective-permute-start.1 = (f32[2048,1280]{1,0:T(8,128)}, f32[2048,1280]{1,0:T(8,128)}, u32[]{:S(2)}, u32[]{:S(2)}) collective-permute-start(f32[2048,1280]{1,0:T(8,128)} %add.180), channel_id=1, source_target_pairs={{0,2},{1,3},{2,0},{3,1},{4,6},{5,7},{6,4},{7,5},{8,10},{9,11},{10,... | collective-permute-start | bytes 31457288 | tf_op jit(solution)/shard_map/ppermute | solution.py:173
  1550.6 11.4 slice-start.12
  1569.0 421.1 %copy-start.51 = (f32[2048]{0:T(1024)S(1)}, f32[2048]{0:T(1024)}, u32[]{:S(2)}) copy-start(f32[2048]{0:T(1024)} %copy-done.50) | copy-start | bytes 24580
  1569.0 421.1 %copy-start.56 = (f32[1280]{0:T(1024)S(1)}, f32[1280]{0:T(1024)}, u32[]{:S(2)}) copy-start(f32[1280]{0:T(1024)} %param.24) | copy-start | bytes 15364
  1570.6 429.4 %slice-start.3 = ((s8[5242880]{0:T(1024)(128)(4,1)}), s8[1048576]{0:T(1024)(128)(4,1)S(1)}, s32[]{:S(2)}) async-start(s8[5242880]{0:T(1024)(128)(4,1)} %bitcast.176), calls=%async_computation.6 | async-start | bytes 2097152
  1570.7 429.2 %copy-start.61 = (f32[2048]{0:T(1024)S(1)}, f32[2048]{0:T(1024)}, u32[]{:S(2)}) copy-start(f32[2048]{0:T(1024)} %copy-done.60) | copy-start | bytes 24580
  1570.7 429.3 %slice-start.4 = ((s8[5242880]{0:T(1024)(128)(4,1)}), s8[4194304]{0:T(1024)(128)(4,1)S(1)}, s32[]{:S(2)}) async-start(s8[5242880]{0:T(1024)(128)(4,1)} %bitcast.176), calls=%async_computation.7 | async-start | bytes 8388608
  1570.7 429.3 %copy-start.54 = (f32[2048]{0:T(1024)S(1)}, f32[2048]{0:T(1024)}, u32[]{:S(2)}) copy-start(f32[2048]{0:T(1024)} %copy-done.53) | copy-start | bytes 24580
  2005.2 10.7 copy-start.62
  2005.3 10.7 copy-start.63
  2005.3 10.7 copy-start.64
  2005.3 10.6 copy-start.73
  (75 other events, 252.0 us)
Sparse Core Ops, SparseCore 0:
  73.1 361.1 all-reduce.6
  481.2 697.6 all-reduce.10
  1568.5 143.3 all-reduce.8
